TPU v7x, 32 devices: a whole 2x2x4 slice. The times are simulated.
32 devices in a mesh: dp: 4 (over z), row: 4 (over y, x), col: 2 (over core).
Axes of the slice: x: 2, y: 2, z: 4, core: 2. Of those that a mesh axis runs over, the one named last changes fastest.
Arguments:
- tokens: bfloat16 [8, 2048, 768], P(('dp', 'col'), 'row'), may hold values from -6 to 6
- cotangent: bfloat16 [8, 2048, 768], P(('dp', 'col'), 'row'), may hold values from -6 to 6
- timesteps: int32 [8], P(('dp', 'col')), may hold values from 0 to 999
- prefix_len: int32 [8], P(('dp', 'col')), may hold values from 204 to 1024, as said below
- time_table: bfloat16 [1000, 768], P('col'), may hold values from -3 to 3
- ln1_gain: float32 [768], replicated, may hold values from 0.25 to 1.75
- ln1_bias: float32 [768], replicated, may hold values from -3 to 3
- w_qkv: bfloat16 [768, 3, 768], P('col', None, 'row'), may hold values from -0.3125 to 0.3125
- w_out: bfloat16 [768, 768], P('col', 'row'), may hold values from -1.75 to 1.75
- out_bias: float32 [768], replicated, may hold values from -3 to 3
- ln2_gain: float32 [768], replicated, may hold values from 0.25 to 1.75
- ln2_bias: float32 [768], replicated, may hold values from -3 to 3
- w_up: bfloat16 [768, 3072], P('col', 'row'), may hold values from -0.21875 to 0.21875
- up_bias: float32 [3072], P('row'), may hold values from -3 to 3
- w_down: bfloat16 [768, 3072], P('col', 'row'), may hold values from -0.109375 to 0.109375
- down_bias: float32 [768], replicated, may hold values from -4 to 4
Outputs:
- layer_out: bfloat16 [8, 2048, 768], P(('dp', 'col'), 'row')
- tokens_grad: float32 [8, 2048, 768], P(('dp', 'col'), 'row')
- table_grad: float32 [1000, 768], P('col')
- ln1_gain_grad: float32 [768], replicated
- ln1_bias_grad: float32 [768], replicated
- qkv_grad: float32 [768, 3, 768], P('col', None, 'row')
- out_grad: float32 [768, 768], P('col', 'row')
- out_bias_grad: float32 [768], replicated
- ln2_gain_grad: float32 [768], replicated
- ln2_bias_grad: float32 [768], replicated
- up_grad: float32 [768, 3072], P('col', 'row')
- up_bias_grad: float32 [3072], P('row')
- down_grad: float32 [768, 3072], P('col', 'row')
- down_bias_grad: float32 [768], replicated
Inputs may be any that keep to these rules, and one draw needn't show every extreme that they name: `prefix_len`: each sequence's prefix length lies between 204 and 1024, and some sequence takes each end.
All inputs are finite; a program needn't handle non-finite values.
Results may differ from a plain program's by a relative error of at most 0.02.
Values may be sent and summed in bfloat16 or wider, within the bound.
A program may use at most 128 MiB of HBM per device.

v0:
```python
import jax
import jax.numpy as jnp
from jax import lax
from jax.sharding import PartitionSpec as P

HD = 64
norm_eps = 1e-05
masked_score = -1e30


def gelu_exact(values):
    return jax.nn.gelu(values, approximate=False)


def gather_rows(values):
    return lax.all_gather(values, "row", axis=1, tiled=True)


def scatter_rows(values):
    return lax.psum_scatter(
        values.astype(jnp.bfloat16), "row", scatter_dimension=1, tiled=True
    ).astype(jnp.float32)


def gather_grads(values):
    return lax.all_gather(values, "row", axis=1, tiled=True)


def scatter_grads(values):
    return lax.psum_scatter(
        values.astype(jnp.bfloat16), "row", scatter_dimension=1, tiled=True
    ).astype(jnp.float32)


def norm_forward(hidden, gain_vec, bias_vec):
    width = hidden.shape[-1]
    average = jnp.sum(hidden, axis=-1, keepdims=True) / width
    variance = jnp.sum(hidden * hidden, axis=-1, keepdims=True) / width - average * average
    inverse = lax.rsqrt(variance + norm_eps)
    centred = (hidden - average) * inverse
    return (centred * gain_vec + bias_vec, centred, inverse)


def norm_backward(grad_out, centred, inverse, gain_vec):
    width = grad_out.shape[-1]
    scaled = grad_out * gain_vec
    first_mean = jnp.sum(scaled, axis=-1, keepdims=True) / width
    second_mean = jnp.sum(scaled * centred, axis=-1, keepdims=True) / width
    grad_in = inverse * (scaled - first_mean - centred * second_mean)
    return (grad_in, jnp.sum(grad_out * centred, axis=(0, 1)), jnp.sum(grad_out, axis=(0, 1)))


def attend_forward(queries, key_rows, values, prefix):
    length = queries.shape[0]
    block_rows = min(512, length)
    score_scale = queries.shape[2] ** (-0.5)
    key_pos = jnp.arange(length, dtype=jnp.int32)

    def one_block(block_index):
        row_start = block_index * block_rows
        query_blk = lax.dynamic_slice_in_dim(queries, row_start, block_rows, 0)
        scores = (
            jnp.einsum("qhd,khd->hqk", query_blk, key_rows, preferred_element_type=jnp.float32)
            * score_scale
        )
        query_pos = row_start + jnp.arange(block_rows, dtype=jnp.int32)
        allowed = (key_pos[None, :] <= query_pos[:, None]) | (key_pos[None, :] < prefix)
        scores = jnp.where(allowed[None], scores, masked_score)
        row_max = jnp.max(scores, axis=2, keepdims=True)
        exponent = jnp.exp(scores - row_max)
        row_total = jnp.sum(exponent, axis=2, keepdims=True)
        soft_low = (exponent / row_total).astype(jnp.bfloat16)
        mixed_blk = jnp.einsum("hqk,khd->qhd", soft_low, values, preferred_element_type=jnp.float32)
        return (mixed_blk, (row_max + jnp.log(row_total))[:, :, 0])

    mixed, logsums = lax.map(one_block, jnp.arange(length // block_rows, dtype=jnp.int32))
    return (mixed.reshape(queries.shape), logsums)


def attend_backward(queries, key_rows, values, mixed, logsums, grad_mixed, prefix):
    length = queries.shape[0]
    block_rows = min(512, length)
    score_scale = queries.shape[2] ** (-0.5)
    key_pos = jnp.arange(length, dtype=jnp.int32)
    delta = jnp.sum(grad_mixed.astype(jnp.float32) * mixed, axis=2)

    def one_block(grads_carry, block_index):
        grad_keys, grad_values = grads_carry
        row_start = block_index * block_rows
        query_blk = lax.dynamic_slice_in_dim(queries, row_start, block_rows, 0)
        grad_blk = lax.dynamic_slice_in_dim(grad_mixed, row_start, block_rows, 0)
        delta_blk = lax.dynamic_slice_in_dim(delta, row_start, block_rows, 0)
        scores = (
            jnp.einsum("qhd,khd->hqk", query_blk, key_rows, preferred_element_type=jnp.float32)
            * score_scale
        )
        query_pos = row_start + jnp.arange(block_rows, dtype=jnp.int32)
        allowed = (key_pos[None, :] <= query_pos[:, None]) | (key_pos[None, :] < prefix)
        scores = jnp.where(allowed[None], scores, masked_score)
        weights_soft = jnp.exp(scores - logsums[block_index][:, :, None])
        grad_soft = jnp.einsum("qhd,khd->hqk", grad_blk, values, preferred_element_type=jnp.float32)
        grad_scores = (weights_soft * (grad_soft - delta_blk.T[:, :, None])).astype(jnp.bfloat16)
        grad_query = (
            jnp.einsum("hqk,khd->qhd", grad_scores, key_rows, preferred_element_type=jnp.float32)
            * score_scale
        )
        grad_keys = (
            grad_keys
            + jnp.einsum("hqk,qhd->khd", grad_scores, query_blk, preferred_element_type=jnp.float32)
            * score_scale
        )
        grad_values = grad_values + jnp.einsum(
            "hqk,qhd->khd",
            weights_soft.astype(jnp.bfloat16),
            grad_blk,
            preferred_element_type=jnp.float32,
        )
        return ((grad_keys, grad_values), grad_query)

    zero_grads = jnp.zeros(key_rows.shape, jnp.float32)
    final_grads, grad_queries = lax.scan(
        one_block, (zero_grads, zero_grads), jnp.arange(length // block_rows, dtype=jnp.int32)
    )
    return jnp.stack([grad_queries.reshape(key_rows.shape), final_grads[0], final_grads[1]], axis=1)


def body(
    tokens,
    cotangent,
    timesteps,
    prefix_len,
    time_table,
    ln1_gain,
    ln1_bias,
    w_qkv,
    w_out,
    out_bias,
    ln2_gain,
    ln2_bias,
    w_up,
    up_bias,
    w_down,
    down_bias,
):
    highest = lax.Precision.HIGHEST
    qkv_full, out_full, up_full, down_full, table_full = (
        lax.all_gather(w_qkv, "col", axis=0, tiled=True),
        lax.all_gather(w_out, "col", axis=0, tiled=True),
        lax.all_gather(w_up, "col", axis=0, tiled=True),
        lax.all_gather(w_down, "col", axis=0, tiled=True),
        lax.all_gather(time_table, "col", axis=0, tiled=True),
    )
    seq_count = tokens.shape[0]
    width_heads = qkv_full.shape[2]
    heads_local = width_heads // HD
    picked = (
        timesteps[:, None] == jnp.arange(table_full.shape[0], dtype=jnp.int32)[None, :]
    ).astype(jnp.float32)
    embed_rows = jnp.dot(picked, table_full.astype(jnp.float32), precision=highest)

    def sequence_forward(seq_item):
        parts_seq, prefix = seq_item
        return attend_forward(parts_seq[:, 0], parts_seq[:, 1], parts_seq[:, 2], prefix)

    def forward_pass(tokens_in):
        hidden0 = tokens_in.astype(jnp.float32) + embed_rows[:, None, :]
        normed1, centred1, inverse1 = norm_forward(hidden0, ln1_gain, ln1_bias)
        full_one = gather_rows(normed1.astype(jnp.bfloat16))
        length = full_one.shape[1]
        project = jnp.einsum(
            "std,dkh->stkh", full_one, qkv_full, preferred_element_type=jnp.float32
        ).astype(jnp.bfloat16)
        parts = project.reshape(seq_count, length, 3, heads_local, HD)
        mixed, logsums = lax.map(sequence_forward, (parts, prefix_len))
        weighted = mixed.reshape(seq_count, length, width_heads).astype(jnp.bfloat16)
        branch = scatter_rows(
            jnp.einsum("sth,dh->std", weighted, out_full, preferred_element_type=jnp.float32)
        )
        hidden1 = hidden0 + (branch + out_bias)
        normed2, centred2, inverse2 = norm_forward(hidden1, ln2_gain, ln2_bias)
        full_two = gather_rows(normed2.astype(jnp.bfloat16))
        inner = (
            jnp.einsum("std,df->stf", full_two, up_full, preferred_element_type=jnp.float32)
            + up_bias
        )
        active = gelu_exact(inner).astype(jnp.bfloat16)
        result = hidden1 + (
            scatter_rows(
                jnp.einsum("stf,df->std", active, down_full, preferred_element_type=jnp.float32)
            )
            + down_bias
        )
        saved = (
            full_one,
            centred1,
            inverse1,
            parts,
            mixed,
            logsums,
            weighted,
            centred2,
            inverse2,
            full_two,
            inner,
            active,
        )
        return (result, saved)

    result, saved = forward_pass(tokens)
    (
        full_one,
        centred1,
        inverse1,
        parts,
        mixed,
        logsums,
        weighted,
        centred2,
        inverse2,
        full_two,
        inner,
        active,
    ) = saved
    length = full_one.shape[1]
    grad_full = gather_grads(cotangent)
    down_grad_full = jnp.einsum(
        "std,stf->df", grad_full, active, preferred_element_type=jnp.float32
    )
    grad_active = jnp.einsum(
        "std,df->stf", grad_full, down_full, preferred_element_type=jnp.float32
    )
    unused_out, gelu_back = jax.vjp(gelu_exact, inner)
    grad_inner = gelu_back(grad_active)[0]
    inner_low = grad_inner.astype(jnp.bfloat16)
    up_grad_full = jnp.einsum(
        "std,stf->df", full_two, inner_low, preferred_element_type=jnp.float32
    )
    grad_normed2 = scatter_grads(
        jnp.einsum("stf,df->std", inner_low, up_full, preferred_element_type=jnp.float32)
    )
    grad_norm_two, ln2_gain_part, ln2_bias_part = norm_backward(
        grad_normed2, centred2, inverse2, ln2_gain
    )
    grad_hidden1 = cotangent.astype(jnp.float32) + grad_norm_two
    grad_branch_full = gather_grads(grad_hidden1.astype(jnp.bfloat16))
    out_grad_full = jnp.einsum(
        "std,sth->dh", grad_branch_full, weighted, preferred_element_type=jnp.float32
    )
    grad_weighted = jnp.einsum(
        "std,dh->sth", grad_branch_full, out_full, preferred_element_type=jnp.float32
    ).astype(jnp.bfloat16)

    def sequence_backward(seq_item):
        parts_seq, mixed_seq, logsum_seq, grad_seq, prefix = seq_item
        return attend_backward(
            parts_seq[:, 0],
            parts_seq[:, 1],
            parts_seq[:, 2],
            mixed_seq,
            logsum_seq,
            grad_seq,
            prefix,
        )

    grad_parts = lax.map(
        sequence_backward,
        (
            parts,
            mixed,
            logsums,
            grad_weighted.reshape(seq_count, length, heads_local, HD),
            prefix_len,
        ),
    )
    grad_project = grad_parts.reshape(seq_count, length, 3, width_heads).astype(jnp.bfloat16)
    qkv_grad_full = jnp.einsum(
        "std,stkh->dkh", full_one, grad_project, preferred_element_type=jnp.float32
    )
    grad_normed1 = scatter_grads(
        jnp.einsum("stkh,dkh->std", grad_project, qkv_full, preferred_element_type=jnp.float32)
    )
    grad_norm_one, ln1_gain_part, ln1_bias_part = norm_backward(
        grad_normed1, centred1, inverse1, ln1_gain
    )
    grad_hidden0 = grad_hidden1 + grad_norm_one
    seq_sums = jnp.sum(grad_hidden0, axis=1)
    table_grad_full = jnp.einsum("sn,sd->nd", picked, seq_sums, precision=highest)
    vectors = lax.psum(
        (
            ln1_gain_part,
            ln1_bias_part,
            jnp.sum(grad_hidden1, axis=(0, 1)),
            ln2_gain_part,
            ln2_bias_part,
            jnp.sum(cotangent.astype(jnp.float32), axis=(0, 1)),
        ),
        ("dp", "row", "col"),
    )
    up_bias_grad = lax.psum(jnp.sum(grad_inner, axis=(0, 1)), ("dp", "col"))
    weights_full = (qkv_grad_full, out_grad_full, up_grad_full, down_grad_full)
    blocks = (
        lax.psum_scatter(
            weights_full[0].astype(jnp.bfloat16), "col", scatter_dimension=0, tiled=True
        ).astype(jnp.float32),
        lax.psum_scatter(
            weights_full[1].astype(jnp.bfloat16), "col", scatter_dimension=0, tiled=True
        ).astype(jnp.float32),
        lax.psum_scatter(
            weights_full[2].astype(jnp.bfloat16), "col", scatter_dimension=0, tiled=True
        ).astype(jnp.float32),
        lax.psum_scatter(
            weights_full[3].astype(jnp.bfloat16), "col", scatter_dimension=0, tiled=True
        ).astype(jnp.float32),
        lax.psum_scatter(
            table_grad_full.astype(jnp.bfloat16), "col", scatter_dimension=0, tiled=True
        ).astype(jnp.float32),
    )
    weight_blocks = (blocks[0], blocks[1], blocks[2], blocks[3])
    weight_blocks = (
        lax.psum(blocks[0].astype(jnp.bfloat16), "dp").astype(jnp.float32),
        lax.psum(blocks[1].astype(jnp.bfloat16), "dp").astype(jnp.float32),
        lax.psum(blocks[2].astype(jnp.bfloat16), "dp").astype(jnp.float32),
        lax.psum(blocks[3].astype(jnp.bfloat16), "dp").astype(jnp.float32),
    )
    table_block = lax.psum(blocks[4].astype(jnp.bfloat16), ("dp", "row")).astype(jnp.float32)
    return (
        result.astype(jnp.bfloat16),
        grad_hidden0,
        table_block,
        vectors[0],
        vectors[1],
        weight_blocks[0],
        weight_blocks[1],
        vectors[2],
        vectors[3],
        vectors[4],
        weight_blocks[2],
        up_bias_grad,
        weight_blocks[3],
        vectors[5],
    )


def solution(mesh):
    placed = (
        P(("dp", "col"), "row", None),
        P(("dp", "col"), "row", None),
        P(("dp", "col")),
        P(("dp", "col")),
        P("col", None),
        P(),
        P(),
        P("col", None, "row"),
        P("col", "row"),
        P(),
        P(),
        P(),
        P("col", "row"),
        P("row"),
        P("col", "row"),
        P(),
    )
    return jax.shard_map(
        body,
        mesh=mesh,
        in_specs=placed,
        out_specs=(
            P(("dp", "col"), "row", None),
            P(("dp", "col"), "row", None),
            P("col", None),
            P(),
            P(),
            P("col", None, "row"),
            P("col", "row"),
            P(),
            P(),
            P(),
            P("col", "row"),
            P("row"),
            P("col", "row"),
            P(),
        ),
        check_vma=False,
    )
```

profile of v0, /device:TPU:0, one launch (start us, length us, event | category | flops | bytes accessed | tf_op | source)
XLA Modules:
  0.0 882.5 jit_solution(11795420427352458064)
XLA Ops:
  8.7 13.4 %all-gather.21.cloned.1.call-done = bf16[2,500,768]{2,1,0:T(8,128)(2,1)} async-done(((bf16[1,500,768]{2,1,0:T(8,128)(2,1)}), bf16[2,500,768]{2,1,0:T(8,128)(2,1)}) %all-gather.21.cloned.1.call-update) | async-done | bytes 1536016 | tf_op jit(solution)/shard_map/all_gather | solution.py:151
  28.0 2.4 all_gather.29
  30.4 40.8 %all-gather.9.cloned.1.call-done = bf16[1,2048,768]{2,1,0:T(8,128)(2,1)} async-done(((bf16[1,512,768]{2,1,0:T(8,128)(2,1)}), bf16[1,2048,768]{2,1,0:T(8,128)(2,1)}) %all-gather.9.cloned.1.call-update) | async-done | bytes 3145744 | tf_op jit(solution)/shard_map/all_gather | solution.py:16
  71.2 3.9 fusion.62
  75.7 91.3 %while.50 = (s32[]{:T(128)}, f32[4,512,3,64]{1,3,2,0:T(8,128)}, f32[4,3,512]{2,1,0:T(4,128)S(1)}, s32[4]{0:T(128)S(1)}, s32[]{:T(128)}, /*index=5*/bf16[2048,3,6...) while((s32[]{:T(128)}, f32[4,512,3,64]{1,3,2,0:T(8,128)}, ...), condition=%wide.region_5.6_spmd.clone.clone.clone, body=%wide.region_2.5_spmd.clone.clone.sunk.clone | while | flops 845153280 | bytes 44169396 | solution.py:76
  78.4 6.0 fusion.182
  84.4 6.8 fusion.183
  91.2 7.4 fusion.184
  101.2 6.0 fusion.182
  107.2 6.8 fusion.183
  114.0 7.4 fusion.184
  124.1 6.0 fusion.182
  130.1 6.8 fusion.183
  136.8 7.4 fusion.184
  146.9 6.0 fusion.182
  152.9 6.8 fusion.183
  159.6 7.3 fusion.184
  170.5 2.7 fusion.64
  174.1 43.3 %reduce-scatter.17.cloned.1.call-done = bf16[1,512,768]{2,1,0:T(8,128)(2,1)} async-done(((bf16[1,2048,768]{2,1,0:T(8,128)(2,1)}), bf16[1,512,768]{2,1,0:T(8,128)(2,1)}) %reduce-scatter.17.cloned.1.call-update) | async-done | bytes 786448 | tf_op jit(solution)/shard_map/reduce_scatter | solution.py:20
  219.1 2.5 add_convert_fusion.1
  223.0 5.0 all-gather.13.cloned.1.call-done
  228.0 47.4 %all-gather.11.cloned.1.call-done = bf16[1,2048,768]{2,1,0:T(8,128)(2,1)} async-done(((bf16[1,512,768]{2,1,0:T(8,128)(2,1)}), bf16[1,2048,768]{2,1,0:T(8,128)(2,1)}) %all-gather.11.cloned.1.call-update) | async-done | bytes 3145744 | tf_op jit(solution)/shard_map/all_gather | solution.py:16
  275.4 19.0 %multiply_convert_fusion.1 = (bf16[2048,768]{1,0:T(8,128)(2,1)}, f32[2048,768]{1,0:T(8,128)}, f32[2048,768]{1,0:T(8,128)}) fusion(f32[768]{0:T(1024)S(1)} %copy-done.41, bf16[768,768]{1,0:T(8,128)(2,1)} %all-gather.13.cloned.1.call-done, bf16[1,2048,768]{2,1,0:T(8,128)(2,1)} %all-gather.11.cloned.1.call-done), kind=kOutput, calls=%fused_computation.54 | convolution fusion | flops 2519728128 | bytes 20057088 | tf_op jit(solution)/shard_map/std,df->stf/dot_general | solution.py:183
  294.4 38.7 %all-gather.17.cloned.1.call-done = bf16[1,2048,768]{2,1,0:T(8,128)(2,1)} async-done(((bf16[1,512,768]{2,1,0:T(8,128)(2,1)}), bf16[1,2048,768]{2,1,0:T(8,128)(2,1)}) %all-gather.17.cloned.1.call-update) | async-done | bytes 3145744 | tf_op jit(solution)/shard_map/all_gather | solution.py:26
  333.1 11.2 %fusion.112 = (f32[768]{0:T(1024)}, bf16[2048,768]{1,0:T(8,128)(2,1)S(1)}) fusion(f32[2048,768]{1,0:T(8,128)} %get-tuple-element.398, bf16[768,768]{1,0:T(8,128)(2,1)} %all-gather.15.cloned.1.call-done, bf16[1,2048,768]{2,1,0:T(8,128)(2,1)} %all-gather.17.cloned.1.call-done, f32[2048,768]{1,0:T(8,128)} %get-tuple-element.410, f32[768]{0:T(1024)S(1)} %copy-done.41), kind=kOutput, calls=%fused_computation.153 | convolution fusion | flops 2441084160 | bytes 20060160 | tf_op jit(solution)/shard_map/std,df->stf/dot_general | solution.py:229
  345.9 4.0 fusion.66
  350.2 6.6 fusion.65
  356.9 37.2 %reduce-scatter.21.cloned.1.call-done = bf16[1,512,768]{2,1,0:T(8,128)(2,1)} async-done(((bf16[1,2048,768]{2,1,0:T(8,128)(2,1)}), bf16[1,512,768]{2,1,0:T(8,128)(2,1)}) %reduce-scatter.21.cloned.1.call-update) | async-done | bytes 786448 | tf_op jit(solution)/shard_map/reduce_scatter | solution.py:30
  394.1 2.7 fusion.86
  396.8 44.2 %reduce-scatter.19.cloned.1.call-done = bf16[1,512,768]{2,1,0:T(8,128)(2,1)} async-done(((bf16[1,2048,768]{2,1,0:T(8,128)(2,1)}), bf16[1,512,768]{2,1,0:T(8,128)(2,1)}) %reduce-scatter.19.cloned.1.call-update) | async-done | bytes 786448 | tf_op jit(solution)/shard_map/reduce_scatter | solution.py:20
  441.1 4.2 fusion.108
  448.5 6.5 fusion.100
  455.1 2.4 copy.45
  457.5 34.1 %all-gather.19.cloned.1.call-done = bf16[1,2048,768]{2,1,0:T(8,128)(2,1)} async-done(((bf16[1,512,768]{2,1,0:T(8,128)(2,1)}), bf16[1,2048,768]{2,1,0:T(8,128)(2,1)}) %all-gather.19.cloned.1.call-update) | async-done | bytes 3145744 | tf_op jit(solution)/shard_map/all_gather | solution.py:26
  491.6 3.9 fusion.68
  495.6 3.1 reshape.475
  498.6 2.6 fusion.88
  501.2 87.8 %while.51 = (s32[]{:T(128)}, f32[2048,3,64]{0,2,1:T(8,128)S(1)}, f32[2048,3,64]{0,2,1:T(8,128)}, bf16[4,512,3,64]{1,3,2,0:T(8,128)(2,1)}, s32[4]{0:T(128)S(1)}, ...) while((s32[]{:T(128)}, f32[2048,3,64]{0,2,1:T(8,128)S(1)}, ...), condition=%wide.region_15.16_spmd.clone.clone.clone, body=%wide.region_14.15_spmd.clone.clone.sunk.clone | while | flops 2048887296 | bytes 79087952 | solution.py:121
  508.2 5.8 fusion.198
  514.0 5.6 multiply_convert_fusion.5
  519.6 2.0 fusion.199
  529.5 6.4 fusion.198
  535.9 5.6 multiply_convert_fusion.5
  541.5 2.0 fusion.199
  551.5 6.4 fusion.198
  557.9 5.6 multiply_convert_fusion.5
  563.5 2.0 fusion.199
  573.4 6.4 fusion.198
  579.8 5.6 multiply_convert_fusion.5
  589.1 3.0 fusion.103
  601.8 6.8 fusion.92
  608.6 4.0 fusion.67
  612.8 2.3 copy.46
  618.8 10.4 %reduce-scatter.25.cloned.1.call-done = bf16[384,768]{1,0:T(8,128)(2,1)} async-done(((bf16[768,768]{1,0:T(8,128)(2,1)}), bf16[384,768]{1,0:T(8,128)(2,1)}) %reduce-scatter.25.cloned.1.call-update) | async-done | bytes 589840 | tf_op jit(solution)/shard_map/reduce_scatter | solution.py:308
  629.3 48.0 %reduce-scatter.23.cloned.1.call-done = bf16[1,512,768]{2,1,0:T(8,128)(2,1)} async-done(((bf16[1,2048,768]{2,1,0:T(8,128)(2,1)}), bf16[1,512,768]{2,1,0:T(8,128)(2,1)}) %reduce-scatter.23.cloned.1.call-update) | async-done | bytes 786448 | tf_op jit(solution)/shard_map/reduce_scatter | solution.py:30
  679.3 2.9 fusion.109
  682.5 4.4 fusion.4
  686.9 2.3 collective-permute-start
  693.0 18.3 %psum.93 = f32[768]{0:T(1024)} all-reduce(f32[768]{0:T(1024)S(1)} %copy-done.37), channel_id=1, replica_groups=mesh['dp'=4,'row'=4,'col'=2] {'dp','col'}, use_global_device_ids=true, to_apply=%region_39.40 | all-reduce | flops 768 | bytes 6144 | tf_op jit(solution)/shard_map/psum | solution.py:299
  711.3 46.5 %all-reduce.9.cloned.1.call-done = (bf16[384,768]{0,1:T(8,128)(2,1)}, bf16[384,3,192]{0,2,1:T(8,128)(2,1)}, bf16[384,192]{0,1:T(8,128)(2,1)}, bf16[384,768]{1,0:T(8,128)(2,1)}) async-done(((bf16[384,768]{0,1:T(8,128)(2,1)}, bf16[384,3,192]{0,2,1:T(8,128)(2,1)}, bf16[384,192]{0,1:T(8,128)(2,1)}, bf16[384,768]{1,0:T(8,128)(2,1)}), (bf16[384,768]{0,1:T(8,128)(2,1)}, bf16[384,3,192]{0,2,1:T(8,128)(2,1)}, ...) | async-done | bytes 1769488 | tf_op jit(solution)/shard_map/psum | solution.py:323
  759.6 2.3 copy.40
  765.0 40.0 %all-reduce.2 = (f32[768]{0:T(1024)}, f32[768]{0:T(1024)}, f32[768]{0:T(1024)}, f32[768]{0:T(1024)}, f32[768]{0:T(1024)}, /*index=5*/f32[768]{0:T(1024)}) all-reduce(f32[768]{0:T(1024)S(1)} %get-tuple-element.333, f32[768]{0:T(1024)S(1)} %get-tuple-element.342, ...), channel_id=1, replica_groups=mesh['dp'=4,'row'=4,'col'=2] {'dp','row','col'}, use_global_device_ids=true, to_apply=%region_23.24 | all-reduce | flops 4608 | bytes 36864 | tf_op jit(solution)/shard_map/psum | solution.py:288
  804.9 68.4 %all-reduce.7.cloned.1.call-done = bf16[500,768]{1,0:T(8,128)(2,1)} async-done(((bf16[500,768]{1,0:T(8,128)(2,1)}), bf16[500,768]{1,0:T(8,128)(2,1)}) %all-reduce.7.cloned.1.call-update) | async-done | bytes 768016 | tf_op jit(solution)/shard_map/psum | solution.py:325
  873.4 2.4 convert_element_type.176
  (243 shorter events, 74.4 us)
Async XLA Ops:
  7.2 17.0 %copy-start = (bf16[1,512,768]{2,1,0:T(8,128)(2,1)S(1)}, bf16[1,512,768]{2,1,0:T(8,128)(2,1)}, u32[]{:S(2)}) copy-start(bf16[1,512,768]{2,1,0:T(8,128)(2,1)} %param.20) | copy-start | bytes 2359300
  7.2 17.4 %copy-start.24 = (f32[768]{0:T(1024)S(1)}, f32[768]{0:T(1024)}, u32[]{:S(2)}) copy-start(f32[768]{0:T(1024)} %param.25) | copy-start | bytes 9220
  7.2 17.4 %copy-start.34 = (f32[768]{0:T(1024)S(1)}, f32[768]{0:T(1024)}, u32[]{:S(2)}) copy-start(f32[768]{0:T(1024)} %param.26) | copy-start | bytes 9220
  7.2 14.9 %all-gather.21.cloned.1.call-start = ((), (), s32[]{:S(2)}) async-start(), calls=%async_computation.20 | async-start | bytes 2322432 | tf_op jit(solution)/shard_map/all_gather | solution.py:151
  7.9 63.2 %all-gather.9.cloned.1.call-start = ((), (), s32[]{:S(2)}) async-start(), calls=%async_computation.8 | async-start | bytes 3932160 | tf_op jit(solution)/shard_map/all_gather | solution.py:16
  8.7 17.3 %copy-start.21 = (bf16[384,192]{0,1:T(8,128)(2,1)S(1)}, bf16[384,192]{0,1:T(8,128)(2,1)}, u32[]{:S(2)}) copy-start(bf16[384,192]{0,1:T(8,128)(2,1)} %param.28) | copy-start | bytes 442372
  23.8 4.2 copy-start.18
  24.1 416.9 %copy-start.19 = (f32[768]{0:T(1024)}, f32[768]{0:T(1024)S(1)}, u32[]{:S(2)}) copy-start(f32[768]{0:T(1024)S(1)} %convolution_reduce_fusion) | copy-start | bytes 9220
  24.6 50.5 %copy-start.26 = (f32[512]{0:T(512)}, f32[512]{0:T(512)S(1)}, u32[]{:S(2)}) copy-start(f32[512]{0:T(512)S(1)} %get-tuple-element.408) | copy-start | bytes 6148
  24.6 50.5 %copy-start.28 = (f32[512]{0:T(512)}, f32[512]{0:T(512)S(1)}, u32[]{:S(2)}) copy-start(f32[512]{0:T(512)S(1)} %get-tuple-element.409) | copy-start | bytes 6148
  25.9 191.5 %reduce-scatter.17.cloned.1.call-start = ((), (), s32[]{:S(2)}) async-start(), calls=%async_computation.9 | async-start | bytes 3932160 | tf_op jit(solution)/shard_map/reduce_scatter | solution.py:20
  30.4 44.7 %copy-start.13 = (bf16[768,3,192]{0,2,1:T(8,128)(2,1)}, bf16[768,3,192]{0,2,1:T(8,128)(2,1)S(1)}, u32[]{:S(2)}) copy-start(bf16[768,3,192]{0,2,1:T(8,128)(2,1)S(1)} %all_gather.29) | copy-start | bytes 2654212
  167.0 6.2 copy-start.15
  173.2 44.2 %copy-start.22 = (f32[768]{0:T(1024)S(1)}, f32[768]{0:T(1024)}, u32[]{:S(2)}) copy-start(f32[768]{0:T(1024)} %param.29) | copy-start | bytes 9220
  173.2 45.8 %copy-start.23 = (f32[768]{0:T(1024)S(1)}, f32[768]{0:T(1024)}, u32[]{:S(2)}) copy-start(f32[768]{0:T(1024)} %param.30) | copy-start | bytes 9220
  173.2 45.8 %copy-start.35 = (f32[768]{0:T(1024)S(1)}, f32[768]{0:T(1024)}, u32[]{:S(2)}) copy-start(f32[768]{0:T(1024)} %param.31) | copy-start | bytes 9220
  173.2 54.8 %all-gather.13.cloned.1.call-start = ((), (), s32[]{:S(2)}) async-start(), calls=%async_computation.11 | async-start | bytes 1769472 | tf_op jit(solution)/shard_map/all_gather | solution.py:149
  173.8 101.6 %copy-start.41 = (f32[768]{0:T(1024)S(1)}, f32[768]{0:T(1024)}, u32[]{:S(2)}) copy-start(f32[768]{0:T(1024)} %param.33) | copy-start | bytes 9220
  173.8 101.6 %all-gather.11.cloned.1.call-start = ((), (), s32[]{:S(2)}) async-start(), calls=%async_computation.10 | async-start | bytes 3932160 | tf_op jit(solution)/shard_map/all_gather | solution.py:16
  221.6 72.8 %all-gather.15.cloned.1.call-start = ((), (), s32[]{:S(2)}) async-start(), calls=%async_computation.12 | async-start | bytes 1769472 | tf_op jit(solution)/shard_map/all_gather | solution.py:150
  222.2 110.9 %all-gather.17.cloned.1.call-start = ((), (), s32[]{:S(2)}) async-start(), calls=%async_computation.14 | async-start | bytes 3932160 | tf_op jit(solution)/shard_map/all_gather | solution.py:26
  222.9 171.2 %reduce-scatter.21.cloned.1.call-start = ((), (), s32[]{:S(2)}) async-start(), calls=%async_computation.15 | async-start | bytes 3932160 | tf_op jit(solution)/shard_map/reduce_scatter | solution.py:30
  333.1 12.8 %copy-start.40 = (bf16[768,768]{1,0:T(8,128)(2,1)S(1)}, bf16[768,768]{1,0:T(8,128)(2,1)}, u32[]{:S(2)}) copy-start(bf16[768,768]{1,0:T(8,128)(2,1)} %all-gather.13.cloned.1.call-done) | copy-start | bytes 3538948
  344.3 1.6 copy-start.42
  350.0 91.1 %reduce-scatter.19.cloned.1.call-start = ((), (), s32[]{:S(2)}) async-start(), calls=%async_computation.13 | async-start | bytes 3932160 | tf_op jit(solution)/shard_map/reduce_scatter | solution.py:20
  356.8 37.3 %copy-start.4 = (bf16[1,512,768]{2,1,0:T(8,128)(2,1)S(1)}, bf16[1,512,768]{2,1,0:T(8,128)(2,1)}, u32[]{:S(2)}) copy-start(bf16[1,512,768]{2,1,0:T(8,128)(2,1)} %reduce-scatter.17.cloned.1.call-done) | copy-start | bytes 2359300
  356.8 84.2 %copy-start.36 = (f32[768]{0:T(1024)S(1)}, f32[768]{0:T(1024)}, u32[]{:S(2)}) copy-start(f32[768]{0:T(1024)} %param.35) | copy-start | bytes 9220
  356.9 134.8 %all-gather.19.cloned.1.call-start = ((), (), s32[]{:S(2)}) async-start(), calls=%async_computation.16 | async-start | bytes 3932160 | tf_op jit(solution)/shard_map/all_gather | solution.py:26
  447.5 165.3 %reduce-scatter.31.cloned.1.call-start = ((), (), s32[]{:S(2)}) async-start(), calls=%async_computation.23 | async-start | bytes 1769472
  457.5 157.6 %reduce-scatter.29.cloned.1.call-start = ((), (), s32[]{:S(2)}) async-start(), calls=%async_computation.22 | async-start | bytes 589824
  508.2 5.8 copy-start.16
  514.0 5.6 copy-start.10
  529.5 6.4 copy-start.16
  535.9 5.6 copy-start.10
  551.5 6.4 copy-start.16
  557.9 5.6 copy-start.10
  573.4 6.4 copy-start.16
  579.8 5.6 copy-start.10
  589.1 3.9 copy-start.12
  594.2 2.4 copy-start.6
  594.3 2.3 copy-start.8
  596.3 20.5 %reduce-scatter.27.cloned.1.call-start = ((), (), s32[]{:S(2)}) async-start(), calls=%async_computation.21 | async-start | bytes 1474560
  596.3 1.9 copy-start.39
  601.7 6.9 copy-start.7
  601.7 6.9 copy-start.9
  601.7 6.9 copy-start.14
  601.7 27.5 %reduce-scatter.25.cloned.1.call-start = ((), (), s32[]{:S(2)}) async-start(), calls=%async_computation.19 | async-start | bytes 1769472 | tf_op jit(solution)/shard_map/reduce_scatter | solution.py:308
  608.5 68.7 %reduce-scatter.23.cloned.1.call-start = ((), (), s32[]{:S(2)}) async-start(), calls=%async_computation.17 | async-start | bytes 3932160 | tf_op jit(solution)/shard_map/reduce_scatter | solution.py:30
  612.7 64.6 %copy-start.1 = (bf16[1,512,768]{2,1,0:T(8,128)(2,1)S(1)}, bf16[1,512,768]{2,1,0:T(8,128)(2,1)}, u32[]{:S(2)}) copy-start(bf16[1,512,768]{2,1,0:T(8,128)(2,1)} %param.20) | copy-start | bytes 2359300
  612.7 64.6 %copy-start.20 = (f32[768]{0:T(1024)S(1)}, f32[768]{0:T(1024)}, u32[]{:S(2)}) copy-start(f32[768]{0:T(1024)} %copy-done.19) | copy-start | bytes 9220
  612.7 64.6 %copy-start.25 = (f32[768]{0:T(1024)S(1)}, f32[768]{0:T(1024)}, u32[]{:S(2)}) copy-start(f32[768]{0:T(1024)} %param.25) | copy-start | bytes 9220
  612.7 64.6 %copy-start.27 = (f32[512]{0:T(512)S(1)}, f32[512]{0:T(512)}, u32[]{:S(2)}) copy-start(f32[512]{0:T(512)} %copy-done.26) | copy-start | bytes 6148
  612.7 64.6 %copy-start.29 = (f32[512]{0:T(512)S(1)}, f32[512]{0:T(512)}, u32[]{:S(2)}) copy-start(f32[512]{0:T(512)} %copy-done.28) | copy-start | bytes 6148
  612.7 66.6 %copy-start.3 = (f32[1,512,768]{2,1,0:T(8,128)S(1)}, f32[1,512,768]{2,1,0:T(8,128)}, u32[]{:S(2)}) copy-start(f32[1,512,768]{2,1,0:T(8,128)} %copy-done.2) | copy-start | bytes 4718596
  612.7 145.1 %all-reduce.9.cloned.1.call-start = ((), (), s32[]{:S(2)}) async-start(), calls=%async_computation.24 | async-start | bytes 3538944 | tf_op jit(solution)/shard_map/psum | solution.py:323
  629.3 244.1 %all-reduce.7.cloned.1.call-start = ((), (), s32[]{:S(2)}) async-start(), calls=%async_computation.18 | async-start | bytes 1548288 | tf_op jit(solution)/shard_map/psum | solution.py:325
  679.3 9.9 %copy-start.38 = (u32[32]{0:T(128)S(1)}, u32[32]{0:T(128)}, u32[]{:S(2)}) copy-start(u32[32]{0:T(128)} %constant.160) | copy-start | bytes 388
  682.5 10.5 %copy-start.37 = (f32[768]{0:T(1024)S(1)}, f32[768]{0:T(1024)}, u32[]{:S(2)}) copy-start(f32[768]{0:T(1024)} %get-tuple-element.411) | copy-start | bytes 9220
  686.9 3.5 collective-permute-start
  693.0 72.0 %copy-start.30 = (f32[768]{0:T(1024)S(1)}, f32[768]{0:T(1024)}, u32[]{:S(2)}) copy-start(f32[768]{0:T(1024)} %get-tuple-element.331) | copy-start | bytes 9220
  693.0 72.0 %copy-start.31 = (f32[768]{0:T(1024)S(1)}, f32[768]{0:T(1024)}, u32[]{:S(2)}) copy-start(f32[768]{0:T(1024)} %get-tuple-element.341) | copy-start | bytes 9220
  693.0 72.0 %copy-start.32 = (f32[768]{0:T(1024)S(1)}, f32[768]{0:T(1024)}, u32[]{:S(2)}) copy-start(f32[768]{0:T(1024)} %get-tuple-element.393) | copy-start | bytes 9220
  693.0 72.0 %copy-start.33 = (f32[768]{0:T(1024)S(1)}, f32[768]{0:T(1024)}, u32[]{:S(2)}) copy-start(f32[768]{0:T(1024)} %get-tuple-element.405) | copy-start | bytes 9220
  757.9 6.0 copy-start.17
  (6 other events, 7.7 us)
Sparse Core Ops, SparseCore 0:
  9.6 12.4 all-gather.20
  26.0 45.1 all-gather.8
  173.4 43.9 reduce-scatter.16
  218.8 9.1 all-gather.12
  230.3 45.1 all-gather.10
  276.8 9.2 all-gather.14
  287.9 45.1 all-gather.16
  350.1 43.9 reduce-scatter.20
  397.1 43.9 reduce-scatter.18
  447.6 43.9 all-gather.18
  494.4 8.6 reduce-scatter.30
  596.4 7.6 reduce-scatter.28
  606.9 9.6 reduce-scatter.26
  619.4 9.8 reduce-scatter.24
  632.1 45.1 reduce-scatter.22
  680.9 76.8 all-reduce.8
  764.4 108.9 all-reduce.6
where the time goes:
time: 892 us; the launch traced here: 882 us
  waiting for transfers between devices  480 us (54%)
  matrix products  196 us (22%)
  other arithmetic  72.5 us (8%)
  blocking collectives  67.1 us (8%)
  local copies, waits for them, and re-layouts  33.4 us (4%)
  between operations  16.1 us (2%)
  loops' own time  14.2 us (2%)
    all_gather x2, waiting for transfers between devices, gather_rows(): return lax.all_gather(values, 'row', axis=1, tiled=True)  88.2 us
    reduce_scatter x2, waiting for transfers between devices, scatter_rows(): lax.psum_scatter(values.astype(jnp.bfloat16), 'row', scatter_dimension=1,...  87.5 us
    reduce_scatter x2, waiting for transfers between devices, scatter_grads(): lax.psum_scatter(values.astype(jnp.bfloat16), 'row', scatter_dimension=1,...  85.2 us
    all_gather x2, waiting for transfers between devices, gather_grads(): return lax.all_gather(values, 'row', axis=1, tiled=True)  72.8 us
    psum x1, waiting for transfers between devices, body(): lax.psum(blocks[4].astype(jnp.bfloat16), ('dp', 'row')).astype(jnp.float32)  68.4 us
    psum x1, waiting for transfers between devices, body(): lax.psum(blocks[3].astype(jnp.bfloat16), 'dp').astype(jnp.float32)  46.5 us
    psum x1, blocking collectives, body(): lax.psum((ln1_gain_part, ln1_bias_part, jnp.sum(grad_hidden1, axis=(0, 1)...  40 us
    dot_general x8, matrix products, one_block(): jnp.einsum('qhd,khd->hqk', query_blk, key_rows, preferred_element_type=jn...  31.4 us
  transfers between devices with their start and end apart: 18, of which 13 were waited for; matrix products, arithmetic and copies ran while one was open for 20% of the time, Pallas kernels for 0%

commit v1 on v0

--- a/solution.py
+++ b/solution.py
@@ -320,7 +320,7 @@
         lax.psum(blocks[0].astype(jnp.bfloat16), "dp").astype(jnp.float32),
         lax.psum(blocks[1].astype(jnp.bfloat16), "dp").astype(jnp.float32),
         lax.psum(blocks[2].astype(jnp.bfloat16), "dp").astype(jnp.float32),
-        lax.psum(blocks[3].astype(jnp.bfloat16), "dp").astype(jnp.float32),
+        jnp.sum(lax.all_gather(blocks[3].astype(jnp.bfloat16), "dp"), axis=0).astype(jnp.float32),
     )
     table_block = lax.psum(blocks[4].astype(jnp.bfloat16), ("dp", "row")).astype(jnp.float32)
     return (

time: 892 us -> 923 us (1.035)
  waiting for transfers between devices: 480 us -> 502 us
    all_gather x0 -> x1, waiting for transfers between devices: none -> 19 us  [body(): lax.all_gather(blocks[3].astype(jnp.bfloat16), 'dp')]
    unnamed x93 -> x83, local copies, waits for them, and re-layouts: 23.4 us -> 21.7 us
  transfers between devices with their start and end apart: 18 -> 19, of which waited for: 13 -> 14; matrix products, arithmetic and copies ran while one was open for 20% -> 20% of each run, Pallas kernels for 0% -> 0%
where the time goes in v1:
time: 923 us; the launch traced here: 913 us
  waiting for transfers between devices  502 us (54%)
  matrix products  197 us (21%)
  other arithmetic  76.2 us (8%)
  blocking collectives  67.5 us (7%)
  local copies, waits for them, and re-layouts  36.7 us (4%)
  between operations  16.7 us (2%)
  loops' own time  14 us (2%)
    all_gather x2, waiting for transfers between devices, gather_rows(): return lax.all_gather(values, 'row', axis=1, tiled=True)  88.2 us
    reduce_scatter x2, waiting for transfers between devices, scatter_rows(): lax.psum_scatter(values.astype(jnp.bfloat16), 'row', scatter_dimension=1,...  87.5 us
    reduce_scatter x2, waiting for transfers between devices, scatter_grads(): lax.psum_scatter(values.astype(jnp.bfloat16), 'row', scatter_dimension=1,...  84.9 us
    all_gather x2, waiting for transfers between devices, gather_grads(): return lax.all_gather(values, 'row', axis=1, tiled=True)  72.7 us
    psum x1, waiting for transfers between devices, body(): lax.psum(blocks[4].astype(jnp.bfloat16), ('dp', 'row')).astype(jnp.float32)  68.7 us
    psum x1, waiting for transfers between devices, body(): lax.psum(blocks[0].astype(jnp.bfloat16), 'dp').astype(jnp.float32)  50.3 us
    psum x1, blocking collectives, body(): lax.psum((ln1_gain_part, ln1_bias_part, jnp.sum(grad_hidden1, axis=(0, 1)...  40.8 us
    dot_general x8, matrix products, one_block(): jnp.einsum('qhd,khd->hqk', query_blk, key_rows, preferred_element_type=jn...  31.4 us
  transfers between devices with their start and end apart: 19, of which 14 were waited for; matrix products, arithmetic and copies ran while one was open for 20% of the time, Pallas kernels for 0%

profile of v1, /device:TPU:0, one launch (start us, length us, event | category | flops | bytes accessed | tf_op | source)
XLA Modules:
  0.0 913.3 jit_solution(2514501907001744736)
XLA Ops:
  8.7 13.4 %all-gather.25.cloned.1.call-done = bf16[2,500,768]{2,1,0:T(8,128)(2,1)} async-done(((bf16[1,500,768]{2,1,0:T(8,128)(2,1)}), bf16[2,500,768]{2,1,0:T(8,128)(2,1)}) %all-gather.25.cloned.1.call-update) | async-done | bytes 1536016 | tf_op jit(solution)/shard_map/all_gather | solution.py:151
  28.0 2.4 all_gather.35
  30.4 40.8 %all-gather.11.cloned.1.call-done = bf16[1,2048,768]{2,1,0:T(8,128)(2,1)} async-done(((bf16[1,512,768]{2,1,0:T(8,128)(2,1)}), bf16[1,2048,768]{2,1,0:T(8,128)(2,1)}) %all-gather.11.cloned.1.call-update) | async-done | bytes 3145744 | tf_op jit(solution)/shard_map/all_gather | solution.py:16
  71.2 3.9 fusion.62
  76.6 91.9 %while.50 = (s32[]{:T(128)}, f32[4,512,3,64]{1,3,2,0:T(8,128)}, f32[4,3,512]{2,1,0:T(4,128)S(1)}, s32[4]{0:T(128)S(1)}, s32[]{:T(128)}, /*index=5*/bf16[2048,3,6...) while((s32[]{:T(128)}, f32[4,512,3,64]{1,3,2,0:T(8,128)}, ...), condition=%wide.region_5.6_spmd.clone.clone.clone, body=%wide.region_2.5_spmd.clone.clone.sunk.clone | while | flops 845153280 | bytes 47315148 | solution.py:76
  79.3 6.0 fusion.182
  85.3 6.8 fusion.183
  92.1 7.4 fusion.184
  102.3 6.0 fusion.182
  108.3 6.8 fusion.183
  115.1 7.4 fusion.184
  125.2 6.0 fusion.182
  131.2 6.8 fusion.183
  138.1 7.4 fusion.184
  148.2 6.0 fusion.182
  154.2 6.8 fusion.183
  161.1 7.4 fusion.184
  170.8 2.7 fusion.64
  174.4 43.2 %reduce-scatter.17.cloned.1.call-done = bf16[1,512,768]{2,1,0:T(8,128)(2,1)} async-done(((bf16[1,2048,768]{2,1,0:T(8,128)(2,1)}), bf16[1,512,768]{2,1,0:T(8,128)(2,1)}) %reduce-scatter.17.cloned.1.call-update) | async-done | bytes 786448 | tf_op jit(solution)/shard_map/reduce_scatter | solution.py:20
  219.3 2.5 add_convert_fusion.1
  223.2 5.1 all-gather.15.cloned.1.call-done
  228.3 47.4 %all-gather.13.cloned.1.call-done = bf16[1,2048,768]{2,1,0:T(8,128)(2,1)} async-done(((bf16[1,512,768]{2,1,0:T(8,128)(2,1)}), bf16[1,2048,768]{2,1,0:T(8,128)(2,1)}) %all-gather.13.cloned.1.call-update) | async-done | bytes 3145744 | tf_op jit(solution)/shard_map/all_gather | solution.py:16
  275.7 19.0 %multiply_convert_fusion.1 = (bf16[2048,768]{1,0:T(8,128)(2,1)}, f32[2048,768]{1,0:T(8,128)}, f32[2048,768]{1,0:T(8,128)}) fusion(f32[768]{0:T(1024)S(1)} %copy-done.37, bf16[768,768]{1,0:T(8,128)(2,1)} %all-gather.15.cloned.1.call-done, bf16[1,2048,768]{2,1,0:T(8,128)(2,1)} %all-gather.13.cloned.1.call-done), kind=kOutput, calls=%fused_computation.54 | convolution fusion | flops 2519728128 | bytes 20057088 | tf_op jit(solution)/shard_map/std,df->stf/dot_general | solution.py:183
  294.7 38.6 %all-gather.19.cloned.1.call-done = bf16[1,2048,768]{2,1,0:T(8,128)(2,1)} async-done(((bf16[1,512,768]{2,1,0:T(8,128)(2,1)}), bf16[1,2048,768]{2,1,0:T(8,128)(2,1)}) %all-gather.19.cloned.1.call-update) | async-done | bytes 3145744 | tf_op jit(solution)/shard_map/all_gather | solution.py:26
  333.4 11.2 %fusion.112 = (f32[768]{0:T(1024)}, bf16[2048,768]{1,0:T(8,128)(2,1)S(1)}) fusion(f32[2048,768]{1,0:T(8,128)} %get-tuple-element.369, bf16[768,768]{1,0:T(8,128)(2,1)} %all-gather.17.cloned.1.call-done, bf16[1,2048,768]{2,1,0:T(8,128)(2,1)} %all-gather.19.cloned.1.call-done, f32[2048,768]{1,0:T(8,128)} %get-tuple-element.381, f32[768]{0:T(1024)S(1)} %copy-done.37), kind=kOutput, calls=%fused_computation.153 | convolution fusion | flops 2441084160 | bytes 20060160 | tf_op jit(solution)/shard_map/std,df->stf/dot_general | solution.py:229
  346.2 4.0 fusion.66
  350.7 6.6 fusion.65
  357.4 37.0 %reduce-scatter.21.cloned.1.call-done = bf16[1,512,768]{2,1,0:T(8,128)(2,1)} async-done(((bf16[1,2048,768]{2,1,0:T(8,128)(2,1)}), bf16[1,512,768]{2,1,0:T(8,128)(2,1)}) %reduce-scatter.21.cloned.1.call-update) | async-done | bytes 786448 | tf_op jit(solution)/shard_map/reduce_scatter | solution.py:30
  394.4 2.7 fusion.86
  397.1 44.2 %reduce-scatter.19.cloned.1.call-done = bf16[1,512,768]{2,1,0:T(8,128)(2,1)} async-done(((bf16[1,2048,768]{2,1,0:T(8,128)(2,1)}), bf16[1,512,768]{2,1,0:T(8,128)(2,1)}) %reduce-scatter.19.cloned.1.call-update) | async-done | bytes 786448 | tf_op jit(solution)/shard_map/reduce_scatter | solution.py:20
  441.3 4.2 fusion.108
  448.7 6.5 fusion.100
  455.3 2.4 copy.43
  457.8 34.1 %all-gather.21.cloned.1.call-done = bf16[1,2048,768]{2,1,0:T(8,128)(2,1)} async-done(((bf16[1,512,768]{2,1,0:T(8,128)(2,1)}), bf16[1,2048,768]{2,1,0:T(8,128)(2,1)}) %all-gather.21.cloned.1.call-update) | async-done | bytes 3145744 | tf_op jit(solution)/shard_map/all_gather | solution.py:26
  491.8 3.9 fusion.68
  495.8 3.1 reshape.475
  498.8 2.6 fusion.88
  501.5 87.6 %while.51 = (s32[]{:T(128)}, f32[2048,3,64]{0,2,1:T(8,128)S(1)}, f32[2048,3,64]{0,2,1:T(8,128)}, bf16[4,512,3,64]{1,3,2,0:T(8,128)(2,1)}, s32[4]{0:T(128)S(1)}, ...) while((s32[]{:T(128)}, f32[2048,3,64]{0,2,1:T(8,128)S(1)}, ...), condition=%wide.region_15.16_spmd.clone.clone.clone, body=%wide.region_14.15_spmd.clone.clone.sunk.clone | while | flops 2048887296 | bytes 79087952 | solution.py:121
  508.2 5.8 fusion.198
  514.0 5.6 multiply_convert_fusion.5
  529.5 6.4 fusion.198
  535.9 5.6 multiply_convert_fusion.5
  551.5 6.4 fusion.198
  557.9 5.6 multiply_convert_fusion.5
  573.4 6.4 fusion.198
  579.8 5.6 multiply_convert_fusion.5
  589.1 3.0 fusion.103
  601.5 6.7 fusion.92
  608.2 5.2 fusion.67
  613.6 2.3 copy.44
  619.7 9.1 reduce-scatter.25.cloned.1.call-done
  628.9 47.9 %reduce-scatter.23.cloned.1.call-done = bf16[1,512,768]{2,1,0:T(8,128)(2,1)} async-done(((bf16[1,2048,768]{2,1,0:T(8,128)(2,1)}), bf16[1,512,768]{2,1,0:T(8,128)(2,1)}) %reduce-scatter.23.cloned.1.call-update) | async-done | bytes 786448 | tf_op jit(solution)/shard_map/reduce_scatter | solution.py:30
  678.8 2.9 fusion.109
  682.0 4.4 fusion.4
  686.4 2.3 collective-permute-start
  692.5 17.9 %psum.86 = f32[768]{0:T(1024)} all-reduce(f32[768]{0:T(1024)S(1)} %copy-done.33), channel_id=1, replica_groups=mesh['dp'=4,'row'=4,'col'=2] {'dp','col'}, use_global_device_ids=true, to_apply=%region_39.40 | all-reduce | flops 768 | bytes 6144 | tf_op jit(solution)/shard_map/psum | solution.py:299
  710.4 19.0 %all-gather.23.cloned.1.call-done = bf16[1536,768]{0,1:T(8,128)(2,1)} async-done(((bf16[384,768]{0,1:T(8,128)(2,1)}), bf16[1536,768]{0,1:T(8,128)(2,1)}) %all-gather.23.cloned.1.call-update) | async-done | bytes 2359312 | tf_op jit(solution)/shard_map/all_gather | solution.py:323
  729.4 4.1 reshape.476
  733.6 3.2 reduce_sum.194
  738.1 50.3 %all-reduce.9.cloned.1.call-done = (bf16[384,3,192]{0,2,1:T(8,128)(2,1)}, bf16[384,192]{0,1:T(8,128)(2,1)}, bf16[384,768]{1,0:T(8,128)(2,1)}) async-done(((bf16[384,3,192]{0,2,1:T(8,128)(2,1)}, bf16[384,192]{0,1:T(8,128)(2,1)}, bf16[384,768]{1,0:T(8,128)(2,1)}), (bf16[384,3,192]{0,2,1:T(8,128)(2,1)}, bf16[384,192]{0,1:T(8,128)(2,1)}, bf16[384,768]{1,0:T(8,128)(2,1)})) %all-reduce.9.cloned.1.call-update) | async-done | bytes 1179664 | tf_op jit(solution)/shard_map/psum | solution.py:320
  792.0 2.2 convert_element_type.184
  794.2 40.8 %all-reduce.2 = (f32[768]{0:T(1024)}, f32[768]{0:T(1024)}, f32[768]{0:T(1024)}, f32[768]{0:T(1024)}, f32[768]{0:T(1024)}, /*index=5*/f32[768]{0:T(1024)}) all-reduce(f32[768]{0:T(1024)S(1)} %get-tuple-element.305, f32[768]{0:T(1024)S(1)} %get-tuple-element.314, ...), channel_id=1, replica_groups=mesh['dp'=4,'row'=4,'col'=2] {'dp','row','col'}, use_global_device_ids=true, to_apply=%region_23.24 | all-reduce | flops 4608 | bytes 36864 | tf_op jit(solution)/shard_map/psum | solution.py:288
  834.9 68.7 %all-reduce.7.cloned.1.call-done = bf16[500,768]{1,0:T(8,128)(2,1)} async-done(((bf16[500,768]{1,0:T(8,128)(2,1)}), bf16[500,768]{1,0:T(8,128)(2,1)}) %all-reduce.7.cloned.1.call-update) | async-done | bytes 768016 | tf_op jit(solution)/shard_map/psum | solution.py:325
  903.7 2.4 convert_element_type.178
  (246 shorter events, 80.4 us)
Async XLA Ops:
  7.2 17.0 %copy-start = (bf16[1,512,768]{2,1,0:T(8,128)(2,1)S(1)}, bf16[1,512,768]{2,1,0:T(8,128)(2,1)}, u32[]{:S(2)}) copy-start(bf16[1,512,768]{2,1,0:T(8,128)(2,1)} %param.20) | copy-start | bytes 2359300
  7.2 17.4 %copy-start.20 = (f32[768]{0:T(1024)S(1)}, f32[768]{0:T(1024)}, u32[]{:S(2)}) copy-start(f32[768]{0:T(1024)} %param.25) | copy-start | bytes 9220
  7.2 17.4 %copy-start.30 = (f32[768]{0:T(1024)S(1)}, f32[768]{0:T(1024)}, u32[]{:S(2)}) copy-start(f32[768]{0:T(1024)} %param.26) | copy-start | bytes 9220
  7.2 14.9 %all-gather.25.cloned.1.call-start = ((), (), s32[]{:S(2)}) async-start(), calls=%async_computation.21 | async-start | bytes 2322432 | tf_op jit(solution)/shard_map/all_gather | solution.py:151
  7.9 63.2 %all-gather.11.cloned.1.call-start = ((), (), s32[]{:S(2)}) async-start(), calls=%async_computation.8 | async-start | bytes 3932160 | tf_op jit(solution)/shard_map/all_gather | solution.py:16
  8.7 17.3 %copy-start.17 = (bf16[384,192]{0,1:T(8,128)(2,1)S(1)}, bf16[384,192]{0,1:T(8,128)(2,1)}, u32[]{:S(2)}) copy-start(bf16[384,192]{0,1:T(8,128)(2,1)} %param.28) | copy-start | bytes 442372
  23.8 4.2 copy-start.14
  24.1 417.2 %copy-start.15 = (f32[768]{0:T(1024)}, f32[768]{0:T(1024)S(1)}, u32[]{:S(2)}) copy-start(f32[768]{0:T(1024)S(1)} %convolution_reduce_fusion) | copy-start | bytes 9220
  24.6 50.5 %copy-start.22 = (f32[512]{0:T(512)}, f32[512]{0:T(512)S(1)}, u32[]{:S(2)}) copy-start(f32[512]{0:T(512)S(1)} %get-tuple-element.379) | copy-start | bytes 6148
  24.6 50.5 %copy-start.24 = (f32[512]{0:T(512)}, f32[512]{0:T(512)S(1)}, u32[]{:S(2)}) copy-start(f32[512]{0:T(512)S(1)} %get-tuple-element.380) | copy-start | bytes 6148
  25.9 191.7 %reduce-scatter.17.cloned.1.call-start = ((), (), s32[]{:S(2)}) async-start(), calls=%async_computation.9 | async-start | bytes 3932160 | tf_op jit(solution)/shard_map/reduce_scatter | solution.py:20
  30.4 44.7 %copy-start.11 = (bf16[768,3,192]{0,2,1:T(8,128)(2,1)}, bf16[768,3,192]{0,2,1:T(8,128)(2,1)S(1)}, u32[]{:S(2)}) copy-start(bf16[768,3,192]{0,2,1:T(8,128)(2,1)S(1)} %all_gather.35) | copy-start | bytes 2654212
  85.3 6.8 copy-start.12
  108.3 6.8 copy-start.12
  131.2 6.8 copy-start.12
  154.2 6.8 copy-start.12
  170.8 2.7 copy-start.5
  173.5 44.1 %copy-start.18 = (f32[768]{0:T(1024)S(1)}, f32[768]{0:T(1024)}, u32[]{:S(2)}) copy-start(f32[768]{0:T(1024)} %param.29) | copy-start | bytes 9220
  173.5 45.8 %copy-start.19 = (f32[768]{0:T(1024)S(1)}, f32[768]{0:T(1024)}, u32[]{:S(2)}) copy-start(f32[768]{0:T(1024)} %param.30) | copy-start | bytes 9220
  173.5 45.8 %copy-start.31 = (f32[768]{0:T(1024)S(1)}, f32[768]{0:T(1024)}, u32[]{:S(2)}) copy-start(f32[768]{0:T(1024)} %param.31) | copy-start | bytes 9220
  173.5 54.7 %all-gather.15.cloned.1.call-start = ((), (), s32[]{:S(2)}) async-start(), calls=%async_computation.11 | async-start | bytes 1769472 | tf_op jit(solution)/shard_map/all_gather | solution.py:149
  174.1 101.6 %copy-start.37 = (f32[768]{0:T(1024)S(1)}, f32[768]{0:T(1024)}, u32[]{:S(2)}) copy-start(f32[768]{0:T(1024)} %param.33) | copy-start | bytes 9220
  174.1 101.6 %all-gather.13.cloned.1.call-start = ((), (), s32[]{:S(2)}) async-start(), calls=%async_computation.10 | async-start | bytes 3932160 | tf_op jit(solution)/shard_map/all_gather | solution.py:16
  221.8 72.9 %all-gather.17.cloned.1.call-start = ((), (), s32[]{:S(2)}) async-start(), calls=%async_computation.12 | async-start | bytes 1769472 | tf_op jit(solution)/shard_map/all_gather | solution.py:150
  222.4 111.0 %all-gather.19.cloned.1.call-start = ((), (), s32[]{:S(2)}) async-start(), calls=%async_computation.14 | async-start | bytes 3932160 | tf_op jit(solution)/shard_map/all_gather | solution.py:26
  223.2 171.2 %reduce-scatter.21.cloned.1.call-start = ((), (), s32[]{:S(2)}) async-start(), calls=%async_computation.15 | async-start | bytes 3932160 | tf_op jit(solution)/shard_map/reduce_scatter | solution.py:30
  333.4 12.8 %copy-start.36 = (bf16[768,768]{1,0:T(8,128)(2,1)S(1)}, bf16[768,768]{1,0:T(8,128)(2,1)}, u32[]{:S(2)}) copy-start(bf16[768,768]{1,0:T(8,128)(2,1)} %all-gather.15.cloned.1.call-done) | copy-start | bytes 3538948
  350.2 91.1 %reduce-scatter.19.cloned.1.call-start = ((), (), s32[]{:S(2)}) async-start(), calls=%async_computation.13 | async-start | bytes 3932160 | tf_op jit(solution)/shard_map/reduce_scatter | solution.py:20
  357.3 37.1 %copy-start.4 = (bf16[1,512,768]{2,1,0:T(8,128)(2,1)S(1)}, bf16[1,512,768]{2,1,0:T(8,128)(2,1)}, u32[]{:S(2)}) copy-start(bf16[1,512,768]{2,1,0:T(8,128)(2,1)} %reduce-scatter.17.cloned.1.call-done) | copy-start | bytes 2359300
  357.3 84.0 %copy-start.32 = (f32[768]{0:T(1024)S(1)}, f32[768]{0:T(1024)}, u32[]{:S(2)}) copy-start(f32[768]{0:T(1024)} %param.35) | copy-start | bytes 9220
  357.3 134.5 %all-gather.21.cloned.1.call-start = ((), (), s32[]{:S(2)}) async-start(), calls=%async_computation.16 | async-start | bytes 3932160 | tf_op jit(solution)/shard_map/all_gather | solution.py:26
  447.7 165.9 %reduce-scatter.31.cloned.1.call-start = ((), (), s32[]{:S(2)}) async-start(), calls=%async_computation.24 | async-start | bytes 1769472
  457.7 158.3 %reduce-scatter.29.cloned.1.call-start = ((), (), s32[]{:S(2)}) async-start(), calls=%async_computation.23 | async-start | bytes 589824
  508.2 5.8 copy-start.13
  514.0 5.6 copy-start.8
  529.5 6.4 copy-start.13
  535.9 5.6 copy-start.8
  551.5 6.4 copy-start.13
  557.9 5.6 copy-start.8
  573.4 6.4 copy-start.13
  579.8 5.6 copy-start.8
  589.1 3.9 copy-start.10
  595.8 4.2 copy-start.6
  595.8 21.9 %reduce-scatter.27.cloned.1.call-start = ((), (), s32[]{:S(2)}) async-start(), calls=%async_computation.22 | async-start | bytes 1474560
  595.9 2.1 copy-start.35
  601.4 6.8 copy-start.7
  601.5 27.3 %reduce-scatter.25.cloned.1.call-start = ((), (), s32[]{:S(2)}) async-start(), calls=%async_computation.19 | async-start | bytes 1769472 | tf_op jit(solution)/shard_map/reduce_scatter | solution.py:308
  608.2 68.6 %reduce-scatter.23.cloned.1.call-start = ((), (), s32[]{:S(2)}) async-start(), calls=%async_computation.17 | async-start | bytes 3932160 | tf_op jit(solution)/shard_map/reduce_scatter | solution.py:30
  613.5 63.3 %copy-start.1 = (bf16[1,512,768]{2,1,0:T(8,128)(2,1)S(1)}, bf16[1,512,768]{2,1,0:T(8,128)(2,1)}, u32[]{:S(2)}) copy-start(bf16[1,512,768]{2,1,0:T(8,128)(2,1)} %param.20) | copy-start | bytes 2359300
  613.5 63.3 %copy-start.16 = (f32[768]{0:T(1024)S(1)}, f32[768]{0:T(1024)}, u32[]{:S(2)}) copy-start(f32[768]{0:T(1024)} %copy-done.15) | copy-start | bytes 9220
  613.5 63.3 %copy-start.21 = (f32[768]{0:T(1024)S(1)}, f32[768]{0:T(1024)}, u32[]{:S(2)}) copy-start(f32[768]{0:T(1024)} %param.25) | copy-start | bytes 9220
  613.5 63.3 %copy-start.23 = (f32[512]{0:T(512)S(1)}, f32[512]{0:T(512)}, u32[]{:S(2)}) copy-start(f32[512]{0:T(512)} %copy-done.22) | copy-start | bytes 6148
  613.5 63.3 %copy-start.25 = (f32[512]{0:T(512)S(1)}, f32[512]{0:T(512)}, u32[]{:S(2)}) copy-start(f32[512]{0:T(512)} %copy-done.24) | copy-start | bytes 6148
  613.5 65.3 %copy-start.3 = (f32[1,512,768]{2,1,0:T(8,128)S(1)}, f32[1,512,768]{2,1,0:T(8,128)}, u32[]{:S(2)}) copy-start(f32[1,512,768]{2,1,0:T(8,128)} %copy-done.2) | copy-start | bytes 4718596
  613.6 115.9 %all-gather.23.cloned.1.call-start = ((), (), s32[]{:S(2)}) async-start(), calls=%async_computation.20 | async-start | bytes 2949120 | tf_op jit(solution)/shard_map/all_gather | solution.py:323
  615.9 172.4 %all-reduce.9.cloned.1.call-start = ((), (), s32[]{:S(2)}) async-start(), calls=%async_computation.25 | async-start | bytes 2359296 | tf_op jit(solution)/shard_map/psum | solution.py:320
  628.8 274.9 %all-reduce.7.cloned.1.call-start = ((), (), s32[]{:S(2)}) async-start(), calls=%async_computation.18 | async-start | bytes 1548288 | tf_op jit(solution)/shard_map/psum | solution.py:325
  678.8 9.9 %copy-start.34 = (u32[32]{0:T(128)S(1)}, u32[32]{0:T(128)}, u32[]{:S(2)}) copy-start(u32[32]{0:T(128)} %constant.162) | copy-start | bytes 388
  682.0 10.5 %copy-start.33 = (f32[768]{0:T(1024)S(1)}, f32[768]{0:T(1024)}, u32[]{:S(2)}) copy-start(f32[768]{0:T(1024)} %get-tuple-element.382) | copy-start | bytes 9220
  686.4 3.5 collective-permute-start
  736.7 57.4 %copy-start.26 = (f32[768]{0:T(1024)S(1)}, f32[768]{0:T(1024)}, u32[]{:S(2)}) copy-start(f32[768]{0:T(1024)} %get-tuple-element.303) | copy-start | bytes 9220
  736.8 57.4 %copy-start.27 = (f32[768]{0:T(1024)S(1)}, f32[768]{0:T(1024)}, u32[]{:S(2)}) copy-start(f32[768]{0:T(1024)} %get-tuple-element.313) | copy-start | bytes 9220
  736.8 57.4 %copy-start.28 = (f32[768]{0:T(1024)S(1)}, f32[768]{0:T(1024)}, u32[]{:S(2)}) copy-start(f32[768]{0:T(1024)} %get-tuple-element.364) | copy-start | bytes 9220
  736.8 57.4 %copy-start.29 = (f32[768]{0:T(1024)S(1)}, f32[768]{0:T(1024)}, u32[]{:S(2)}) copy-start(f32[768]{0:T(1024)} %get-tuple-element.376) | copy-start | bytes 9220
  (6 other events, 8.4 us)
Sparse Core Ops, SparseCore 0:
  9.6 12.4 all-gather.24
  26.0 45.1 all-gather.10
  173.7 43.9 reduce-scatter.16
  219.0 9.2 all-gather.14
  230.5 45.1 all-gather.12
  277.1 9.2 all-gather.16
  288.2 45.1 all-gather.18
  350.4 43.9 reduce-scatter.20
  397.4 43.9 reduce-scatter.18
  447.8 43.9 all-gather.20
  494.6 8.6 reduce-scatter.30
  596.0 7.6 reduce-scatter.28
  606.5 9.6 reduce-scatter.26
  618.9 9.8 reduce-scatter.24
  631.6 45.1 reduce-scatter.22
  678.8 50.5 all-gather.22
  733.0 55.3 all-reduce.8
  794.1 109.5 all-reduce.6
